TPU v7x, 32 devices: a whole 2x2x4 slice. The times are simulated.
32 devices in a mesh: dp: 16 (over z, y, core), mp: 2 (over x).
Axes of the slice: x: 2, y: 2, z: 4, core: 2. Of those that a mesh axis runs over, the one named last changes fastest.
Arguments:
- inputs: bfloat16 [8192, 2048], P('dp', 'mp'), may hold values from -6 to 6
- grad_moved: bfloat16 [8192, 2048], P('dp', 'mp'), may hold values from -6 to 6
- moved: int32 [16, 4], P('dp'), may hold values from 0 to 1, as said below
- segments: int32 [8192], P('dp'), may hold values from 0 to 511, as said below
- input_norm_gain: float32 [2048], replicated, may hold values from 0.5 to 1.5
- proj_in: bfloat16 [2048, 3072], P(None, 'mp'), may hold values from -0.125 to 0.125
- proj_out: bfloat16 [1024, 2048], P('mp'), may hold values from -0.1875 to 0.1875
Outputs:
- input_gradient: bfloat16 [8192, 2048], P('dp', 'mp')
- grad_proj_in: float32 [2048, 3072], P('dp', 'mp')
- grad_proj_out: float32 [1024, 2048], P('mp', 'dp')
Inputs may be any that keep to these rules, and one draw needn't show every extreme that they name: moved[g] equals moved[g XOR (8)] for every group g: blocks are swapped between partner groups slot for slot. `segments`: within each group of 512 rows the history numbers start at 0 on its first row, never fall and rise by at most one from row to row; histories never cross groups; in some group every event is a history of its own.
All inputs are finite; a program needn't handle non-finite values.
Results may differ from a plain program's by a relative error of at most 0.011.
Values may be sent and summed in bfloat16 or wider, within the bound.
A program may use at most 128 MiB of HBM per device.

v0:
```python
import jax
import jax.numpy as jnp
from jax import lax
from jax.sharding import PartitionSpec as P

DV = 128
DQK = 64
BLOCK = 128
epsilon = 1e-05
head_floor = 1.0


def swapped(block, axis, apart):
    count = lax.axis_size(axis)
    route = []
    for low in range(count):
        high = low | 1 << apart
        if high != low and high < count:
            route += [(low, high), (high, low)]
    return lax.ppermute(block, axis, route)


def forward_heads(acts, visible, heads_here):
    span = 2 * DV + 2 * DQK
    rows = acts.shape[0]
    parts = acts.reshape(rows, heads_here, span)
    u_vals = parts[:, :, :DV]
    v_vals = parts[:, :, DV : 2 * DV]
    q_vals = parts[:, :, 2 * DV : 2 * DV + DQK]
    k_vals = parts[:, :, 2 * DV + DQK :]
    scores = jnp.einsum("qhd,khd->hqk", q_vals, k_vals, preferred_element_type=jnp.float32)
    sig_s = jax.nn.sigmoid(scores)
    attend = (scores * sig_s * visible[None]).astype(jnp.bfloat16)
    slope = sig_s * (1.0 + scores * (1.0 - sig_s))
    outvals = jnp.einsum("hqk,khd->qhd", attend, v_vals, preferred_element_type=jnp.float32)
    mean_shifted = outvals - jnp.mean(outvals, axis=-1, keepdims=True)
    head_inv = lax.rsqrt(jnp.mean(mean_shifted * mean_shifted, axis=-1, keepdims=True) + head_floor)
    onorm = mean_shifted * head_inv
    mixed = (onorm * u_vals).astype(jnp.bfloat16).reshape(rows, heads_here * DV)
    saved = (u_vals, v_vals, q_vals, k_vals, attend, slope, onorm, head_inv)
    return (mixed, saved)


def backward_heads(saved, grad_mix, visible, heads_here):
    u_vals, v_vals, q_vals, k_vals, attend, slope, onorm, head_inv = saved
    rows = grad_mix.shape[0]
    grad_mixr = grad_mix.reshape(rows, heads_here, DV)
    grad_u = grad_mixr * onorm
    gon = grad_mixr * u_vals
    grad_o = (
        head_inv
        * (
            gon
            - jnp.mean(gon, axis=-1, keepdims=True)
            - onorm * jnp.mean(gon * onorm, axis=-1, keepdims=True)
        )
    ).astype(jnp.bfloat16)
    grad_att = jnp.einsum("qhd,khd->hqk", grad_o, v_vals, preferred_element_type=jnp.float32)
    grad_v = jnp.einsum("hqk,qhd->khd", attend, grad_o, preferred_element_type=jnp.float32)
    grad_scores = (grad_att * visible[None] * slope).astype(jnp.bfloat16)
    grad_q = jnp.einsum("hqk,khd->qhd", grad_scores, k_vals, preferred_element_type=jnp.float32)
    grad_k = jnp.einsum("hqk,qhd->khd", grad_scores, q_vals, preferred_element_type=jnp.float32)
    grad_act = jnp.concatenate([grad_u, grad_v, grad_q, grad_k], axis=-1)
    return grad_act.reshape(rows, heads_here * (2 * DV + 2 * DQK))


def on_device(inputs, grad_moved, moved, segments, input_norm_gain, proj_in, proj_out):
    rows = inputs.shape[0]
    span = 2 * DV + 2 * DQK
    heads_here = proj_in.shape[1] // span
    top_bit = lax.axis_size("dp").bit_length() - 2
    partner = swapped(grad_moved, "dp", top_bit)
    blocks = rows // BLOCK
    flags = moved[0][:, None, None] == 1
    returned = jnp.where(
        flags, partner.reshape(blocks, BLOCK, -1), grad_moved.reshape(blocks, BLOCK, -1)
    ).reshape(rows, -1)
    full_x, full_dy = (
        lax.all_gather(inputs, "mp", axis=1, tiled=True),
        lax.all_gather(returned, "mp", axis=1, tiled=True),
    )
    xfull = full_x.astype(jnp.float32)
    mean_shifted = xfull - jnp.mean(xfull, axis=1, keepdims=True)
    inverse_deviation = lax.rsqrt(
        jnp.mean(mean_shifted * mean_shifted, axis=1, keepdims=True) + epsilon
    )
    standardized_input = mean_shifted * inverse_deviation
    normalized_rows = (standardized_input * input_norm_gain[None, :]).astype(jnp.bfloat16)
    pre = jnp.dot(normalized_rows, proj_in, preferred_element_type=jnp.float32)
    sig_p = jax.nn.sigmoid(pre)
    acts = (pre * sig_p).astype(jnp.bfloat16)
    grad_mix = lax.dot_general(
        full_dy, proj_out, (((1,), (1,)), ((), ())), preferred_element_type=jnp.float32
    )
    order = jnp.arange(rows, dtype=jnp.int32)
    visible = (
        (segments[:, None] == segments[None, :]) & (order[None, :] <= order[:, None])
    ).astype(jnp.float32)
    mixed, saved = forward_heads(acts, visible, heads_here)
    grad_act = backward_heads(saved, grad_mix, visible, heads_here)
    partial_out = lax.dot_general(
        mixed, full_dy, (((0,), (0,)), ((), ())), preferred_element_type=jnp.float32
    )
    grad_proj_out = lax.psum_scatter(partial_out, "dp", scatter_dimension=1, tiled=True)
    grad_pre = (grad_act * sig_p * (1.0 + pre * (1.0 - sig_p))).astype(jnp.bfloat16)
    partial_in = lax.dot_general(
        normalized_rows, grad_pre, (((0,), (0,)), ((), ())), preferred_element_type=jnp.float32
    )
    grad_proj_in = lax.psum_scatter(partial_in, "dp", scatter_dimension=0, tiled=True)
    normed_term = lax.dot_general(
        grad_pre, proj_in, (((1,), (1,)), ((), ())), preferred_element_type=jnp.float32
    )
    local = inputs.shape[1]
    offset = lax.axis_index("mp") * local
    grad_normed = lax.psum(normed_term.astype(jnp.bfloat16), "mp").astype(jnp.float32)
    gain_scaled = grad_normed * input_norm_gain[None, :]
    grad_full = full_dy.astype(jnp.float32) + inverse_deviation * (
        gain_scaled
        - jnp.mean(gain_scaled, axis=1, keepdims=True)
        - standardized_input * jnp.mean(gain_scaled * standardized_input, axis=1, keepdims=True)
    )
    input_gradient = lax.dynamic_slice_in_dim(grad_full, offset, local, 1).astype(jnp.bfloat16)
    return (input_gradient, grad_proj_in, grad_proj_out)


def solution(mesh):
    return jax.shard_map(
        on_device,
        mesh=mesh,
        in_specs=(
            P("dp", "mp"),
            P("dp", "mp"),
            P("dp", None),
            P("dp"),
            P(),
            P(None, "mp"),
            P("mp", None),
        ),
        out_specs=(P("dp", "mp"), P("dp", "mp"), P("mp", "dp")),
        check_vma=False,
    )
```

profile of v0, /device:TPU:0, one launch (start us, length us, event | category | flops | bytes accessed | tf_op | source)
XLA Modules:
  0.0 408.2 jit_solution(3940126649149491493)
XLA Ops:
  7.2 0.0 all-gather.5.cloned.1.call-start
  7.2 0.7 all-gather.5.cloned.1.call-update
  7.9 0.0 all-gather.3.cloned.1.call-start
  8.0 4.1 %collective-permute-start = (bf16[512,1024]{1,0:T(8,128)(2,1)}, bf16[512,1024]{1,0:T(8,128)(2,1)S(1)}, u32[]{:S(2)}, u32[]{:S(2)}) collective-permute-start(bf16[512,1024]{1,0:T(8,128)(2,1)} %param.8), channel_id=1, source_target_pairs={{0,16},{16,0},{2,18},{18,2},{4,20},{20,4},{6,22},{22,6},{8,24},{24... | collective-permute-start | bytes 3145736 | tf_op jit(solution)/shard_map/ppermute | solution.py:20
  12.1 0.7 compare_bitcast_fusion
  12.8 0.1 broadcast_bitcast_fusion
  12.8 0.9 fusion.10
  13.8 44.2 %collective-permute-done = bf16[512,1024]{1,0:T(8,128)(2,1)S(1)} collective-permute-done((bf16[512,1024]{1,0:T(8,128)(2,1)}, bf16[512,1024]{1,0:T(8,128)(2,1)S(1)}, u32[]{:S(2)}, u32[]{:S(2)}) %collective-permute-start) | collective-permute-done | bytes 1048608 | tf_op jit(solution)/shard_map/ppermute | solution.py:20
  57.9 2.4 broadcast_select_fusion
  60.3 0.0 all-gather.3.cloned.1.call-update
  60.4 0.0 all-reduce.2.cloned.1.call-start
  60.4 0.0 all-gather.5.cloned.1.call-done
  60.5 2.1 convert_reduce_fusion
  62.6 0.1 copy-done.2
  62.7 0.7 fusion.2
  63.4 8.2 %multiply_convert_fusion.4 = (bf16[512,1536]{1,0:T(8,128)(2,1)}, f32[512,1536]{1,0:T(8,128)}) fusion(bf16[2048,1536]{1,0:T(8,128)(2,1)} %param.12, f32[2048]{0:T(1024)S(1)} %copy-done.13, f32[512]{0:T(512)S(1)} %add_rsqrt_fusion.1, f32[512]{0:T(512)S(1)} %broadcast_multiply_fusion.5, bf16[512,2048]{1,0:T(8,128)(2,1)S(1)} %copy-done.2), kind=kOutput, calls=%fused_computation.13 | convolution fusion | flops 3230400512 | bytes 13119488 | tf_op jit(solution)/shard_map/dot_general | solution.py:89
  71.5 2.6 copy.20
  74.1 4.3 %multiply_convert_fusion.1 = (bf16[4,512,512]{2,1,0:T(8,128)(2,1)S(1)}, f32[4,512,512]{2,1,0:T(8,128)}) fusion(f32[512,512]{1,0:T(8,128)S(1)} %fusion.10, bf16[512,4,384]{0,2,1:T(8,128)(2,1)} %bitcast.35), kind=kOutput, calls=%fused_computation.8 | convolution fusion | flops 140509184 | bytes 7864320 | tf_op jit(solution)/shard_map/qhd,khd->hqk/dot_general | solution.py:31
  78.4 1.4 copy-done.5
  79.8 1.9 fusion.24
  81.7 0.1 multiply_reduce_fusion.2
  81.8 13.0 %all-gather.3.cloned.1.call-done = bf16[512,2048]{1,0:T(8,128)(2,1)} async-done(((bf16[512,1024]{1,0:T(8,128)(2,1)}), bf16[512,2048]{1,0:T(8,128)(2,1)}) %all-gather.3.cloned.1.call-update) | async-done | bytes 2097168 | tf_op jit(solution)/shard_map/all_gather | solution.py:80
  94.8 3.0 fusion.25
  97.8 1.2 fusion.16
  99.0 0.4 multiply_convert_fusion.5
  99.4 1.1 copy-done.14
  100.5 2.1 multiply_convert_fusion
  102.6 0.5 convolution_bitcast_fusion.2
  103.1 0.7 convolution_bitcast_fusion.3
  103.8 0.4 copy-done.6
  104.2 0.4 convolution_bitcast_fusion
  104.6 2.0 pad_maximum_fusion
  106.6 3.5 copy.19
  110.1 3.9 multiply_convert_fusion.3
  114.1 1.1 copy-done.10
  115.2 7.7 %convolution_convert_fusion = bf16[512,2048]{1,0:T(8,128)(2,1)} fusion(bf16[512,1536]{1,0:T(8,128)(2,1)S(1)} %multiply_convert_fusion.3, bf16[2048,1536]{1,0:T(8,128)(2,1)} %param.12), kind=kOutput, calls=%fused_computation.15 | convolution fusion | flops 3222274048 | bytes 9961472 | tf_op jit(solution)/shard_map/dot_general | solution.py:110
  122.9 0.0 all-reduce.2.cloned.1.call-update
  122.9 0.2 reduce-scatter.5.cloned.1.call-start
  123.2 3.2 fusion.26
  126.4 0.0 reduce-scatter.3.cloned.1.call-start
  126.5 1.5 copy-done.3
  128.0 8.4 %fusion.11 = f32[2048,1536]{1,0:T(8,128)} fusion(bf16[512,1536]{1,0:T(8,128)(2,1)} %copy-done.10, f32[2048]{0:T(1024)S(1)} %copy-done.13, bf16[512,2048]{1,0:T(8,128)(2,1)S(1)} %copy-done.3, f32[512]{0:T(512)S(1)} %add_rsqrt_fusion.1, f32[512]{0:T(512)S(1)} %broadcast_multiply_fusion.5), kind=kOutput, calls=%fused_computation.38 | convolution fusion | flops 3226468352 | bytes 16265216 | tf_op jit(solution)/shard_map/dot_general | solution.py:106
  136.4 0.0 reduce-scatter.3.cloned.1.call-update
  136.4 49.7 %all-reduce.2.cloned.1.call-done = bf16[512,2048]{1,0:T(8,128)(2,1)} async-done(((bf16[512,2048]{1,0:T(8,128)(2,1)}), bf16[512,2048]{1,0:T(8,128)(2,1)}) %all-reduce.2.cloned.1.call-update) | async-done | bytes 2097168 | tf_op jit(solution)/shard_map/psum | solution.py:115
  186.1 3.0 fusion.7
  189.2 1.5 fusion.6
  190.7 72.5 %reduce-scatter.5.cloned.1.call-done = f32[512,128]{1,0:T(8,128)} async-done(((f32[512,2048]{1,0:T(8,128)}), f32[512,128]{1,0:T(8,128)}) %reduce-scatter.5.cloned.1.call-update) | async-done | bytes 262160 | tf_op jit(solution)/shard_map/reduce_scatter | solution.py:104
  263.1 138.5 %reduce-scatter.3.cloned.1.call-done = f32[128,1536]{1,0:T(8,128)} async-done(((f32[2048,1536]{1,0:T(8,128)}), f32[128,1536]{1,0:T(8,128)}) %reduce-scatter.3.cloned.1.call-update) | async-done | bytes 786448 | tf_op jit(solution)/shard_map/reduce_scatter | solution.py:109
  (32 shorter events, 0.1 us)
Async XLA Ops:
  7.2 87.6 %copy-start = (bf16[512,2048]{1,0:T(8,128)(2,1)S(1)}, bf16[512,2048]{1,0:T(8,128)(2,1)}, u32[]{:S(2)}) copy-start(bf16[512,2048]{1,0:T(8,128)(2,1)} %param.13) | copy-start | bytes 6291460
  7.2 53.3 %all-gather.5.cloned.1.call-start = ((), (), s32[]{:S(2)}) async-start(), calls=%async_computation.3 | async-start | bytes 3145728 | tf_op jit(solution)/shard_map/all_gather | solution.py:79
  7.9 86.9 %all-gather.3.cloned.1.call-start = ((), (), s32[]{:S(2)}) async-start(), calls=%async_computation.2 | async-start | bytes 3145728 | tf_op jit(solution)/shard_map/all_gather | solution.py:80
  8.0 50.0 %collective-permute-start = (bf16[512,1024]{1,0:T(8,128)(2,1)}, bf16[512,1024]{1,0:T(8,128)(2,1)S(1)}, u32[]{:S(2)}, u32[]{:S(2)}) collective-permute-start(bf16[512,1024]{1,0:T(8,128)(2,1)} %param.8), channel_id=1, source_target_pairs={{0,16},{16,0},{2,18},{18,2},{4,20},{20,4},{6,22},{22,6},{8,24},{24... | collective-permute-start | bytes 3145736 | tf_op jit(solution)/shard_map/ppermute | solution.py:20
  13.8 60.4 %copy-start.11 = (f32[512,512]{1,0:T(8,128)}, f32[512,512]{1,0:T(8,128)S(1)}, u32[]{:S(2)}) copy-start(f32[512,512]{1,0:T(8,128)S(1)} %fusion.10) | copy-start | bytes 3145732
  60.3 3.0 copy-start.13
  60.4 125.7 %all-reduce.2.cloned.1.call-start = ((), (), s32[]{:S(2)}) async-start(), calls=%async_computation.4 | async-start | bytes 4194304 | tf_op jit(solution)/shard_map/psum | solution.py:115
  60.4 2.2 copy-start.2
  78.4 1.4 copy-start.5
  94.8 3.0 copy-start.4
  97.8 1.6 copy-start.12
  97.8 2.7 copy-start.14
  102.6 1.6 copy-start.6
  114.1 1.1 copy-start.10
  115.2 8.0 %copy-start.7 = (bf16[512,2048]{1,0:T(8,128)(2,1)S(1)}, bf16[512,2048]{1,0:T(8,128)(2,1)}, u32[]{:S(2)}) copy-start(bf16[512,2048]{1,0:T(8,128)(2,1)} %all-gather.3.cloned.1.call-done) | copy-start | bytes 6291460
  115.2 8.0 %copy-start.9 = (bf16[512,4,128]{0,2,1:T(8,128)(2,1)S(1)}, bf16[512,4,128]{0,2,1:T(8,128)(2,1)}, u32[]{:S(2)}) copy-start(bf16[512,4,128]{0,2,1:T(8,128)(2,1)} %get-tuple-element.7) | copy-start | bytes 1572868
  122.9 140.2 %reduce-scatter.5.cloned.1.call-start = ((), (), s32[]{:S(2)}) async-start(), calls=%async_computation.6 | async-start | bytes 4456448 | tf_op jit(solution)/shard_map/reduce_scatter | solution.py:104
  126.4 1.6 copy-start.3
  126.4 275.3 %reduce-scatter.3.cloned.1.call-start = ((), (), s32[]{:S(2)}) async-start(), calls=%async_computation.5 | async-start | bytes 13369344 | tf_op jit(solution)/shard_map/reduce_scatter | solution.py:109
  186.1 3.1 copy-start.8
  189.1 212.5 %copy-start.1 = (bf16[512,2048]{1,0:T(8,128)(2,1)S(1)}, bf16[512,2048]{1,0:T(8,128)(2,1)}, u32[]{:S(2)}) copy-start(bf16[512,2048]{1,0:T(8,128)(2,1)} %param.13) | copy-start | bytes 6291460
Sparse Core Ops, SparseCore 0:
  9.5 35.8 all-gather.4
  60.5 34.2 all-gather.2
  123.1 62.9 all-reduce.1
  190.4 72.7 reduce-scatter.4
  267.6 134.0 reduce-scatter.2
where the time goes:
time: 409 us; the launch traced here: 408 us
  waiting for transfers between devices  319 us (78%)
  matrix products  40.3 us (10%)
  other arithmetic  19 us (5%)
  between operations  14 us (3%)
  local copies, waits for them, and re-layouts  11.9 us (3%)
  starting transfers between devices  4.51 us (1%)
    reduce_scatter x1, waiting for transfers between devices, on_device(): lax.psum_scatter(partial_in, 'dp', scatter_dimension=0, tiled=True)  139 us
    reduce_scatter x1, waiting for transfers between devices, on_device(): lax.psum_scatter(partial_out, 'dp', scatter_dimension=1, tiled=True)  72.5 us
    psum x1, waiting for transfers between devices, on_device(): lax.psum(normed_term.astype(jnp.bfloat16), 'mp').astype(jnp.float32)  49.7 us
    ppermute x1, waiting for transfers between devices, swapped(): return lax.ppermute(block, axis, route)  44.2 us
    all_gather x1, waiting for transfers between devices, on_device(): lax.all_gather(returned, 'mp', axis=1, tiled=True)  13 us
    dot_general x1, matrix products, on_device(): lax.dot_general(normalized_rows, grad_pre, (((0,), (0,)), ((), ())), pref...  8.41 us
  transfers between devices with their start and end apart: 6, of which 5 were waited for; matrix products, arithmetic and copies ran while one was open for 10% of the time, Pallas kernels for 0%

commit v1 on v0

--- a/solution.py
+++ b/solution.py
@@ -8,6 +8,10 @@
 BLOCK = 128
 epsilon = 1e-05
 head_floor = 1.0
+
+
+def bring_block(inner_x):
+    return lax.all_gather(inner_x, axis_name="mp").sum(axis=0)
 
 
 def swapped(block, axis, apart):
@@ -112,7 +116,7 @@
     )
     local = inputs.shape[1]
     offset = lax.axis_index("mp") * local
-    grad_normed = lax.psum(normed_term.astype(jnp.bfloat16), "mp").astype(jnp.float32)
+    grad_normed = bring_block(normed_term.astype(jnp.bfloat16)).astype(jnp.float32)
     gain_scaled = grad_normed * input_norm_gain[None, :]
     grad_full = full_dy.astype(jnp.float32) + inverse_deviation * (
         gain_scaled

time: 409 us -> 402 us (0.983)
  waiting for transfers between devices: 319 us -> 307 us
  other arithmetic: 19 us -> 24.1 us
    psum x1 -> x0, waiting for transfers between devices: 49.7 us -> none  [on_device(): lax.psum(normed_term.astype(jnp.bfloat16), 'mp').astype(jnp.float32)]
    all_gather x0 -> x1, waiting for transfers between devices: none -> 43.3 us  [bring_block(): return lax.all_gather(inner_x, axis_name='mp').sum(axis=0)]
    reduce_sum x0 -> x1, other arithmetic: none -> 5.09 us  [bring_block(): return lax.all_gather(inner_x, axis_name='mp').sum(axis=0)]
    reduce_scatter x1, waiting for transfers between devices: 72.5 us -> 67.5 us  [on_device(): lax.psum_scatter(partial_out, 'dp', scatter_dimension=1, tiled=True)]
  transfers between devices with their start and end apart: 6 -> 6, of which waited for: 5 -> 5; matrix products, arithmetic and copies ran while one was open for 10% -> 11% of each run, Pallas kernels for 0% -> 0%
where the time goes in v1:
time: 402 us
  waiting for transfers between devices  307 us (76%)
  matrix products  40.5 us (10%)
  other arithmetic  24.1 us (6%)
  between operations  14 us (3%)
  local copies, waits for them, and re-layouts  12 us (3%)
  starting transfers between devices  4.51 us (1%)
    reduce_scatter x1, waiting for transfers between devices, on_device(): lax.psum_scatter(partial_in, 'dp', scatter_dimension=0, tiled=True)  138 us
    reduce_scatter x1, waiting for transfers between devices, on_device(): lax.psum_scatter(partial_out, 'dp', scatter_dimension=1, tiled=True)  67.5 us
    ppermute x1, waiting for transfers between devices, swapped(): return lax.ppermute(block, axis, route)  44.2 us
    all_gather x1, waiting for transfers between devices, bring_block(): return lax.all_gather(inner_x, axis_name='mp').sum(axis=0)  43.3 us
    all_gather x1, waiting for transfers between devices, on_device(): lax.all_gather(returned, 'mp', axis=1, tiled=True)  12.9 us
    dot_general x1, matrix products, on_device(): lax.dot_general(normalized_rows, grad_pre, (((0,), (0,)), ((), ())), pref...  8.55 us
    dot_general x1, matrix products, on_device(): pre = jnp.dot(normalized_rows, proj_in, preferred_element_type=jnp.float32)  8.21 us
  transfers between devices with their start and end apart: 6, of which 5 were waited for; matrix products, arithmetic and copies ran while one was open for 11% of the time, Pallas kernels for 0%

profile of v1, /device:TPU:0, one launch (start us, length us, event | category | flops | bytes accessed | tf_op | source)
XLA Modules:
  0.0 402.0 jit_solution(5214671095609699421)
XLA Ops:
  7.2 0.0 all-gather.7.cloned.1.call-start
  7.2 0.7 all-gather.7.cloned.1.call-update
  7.9 0.0 all-gather.5.cloned.1.call-start
  8.0 4.1 %collective-permute-start = (bf16[512,1024]{1,0:T(8,128)(2,1)}, bf16[512,1024]{1,0:T(8,128)(2,1)S(1)}, u32[]{:S(2)}, u32[]{:S(2)}) collective-permute-start(bf16[512,1024]{1,0:T(8,128)(2,1)} %param.8), channel_id=1, source_target_pairs={{0,16},{16,0},{2,18},{18,2},{4,20},{20,4},{6,22},{22,6},{8,24},{24... | collective-permute-start | bytes 3145736 | tf_op jit(solution)/shard_map/ppermute | solution.py:24
  12.1 0.7 compare_bitcast_fusion
  12.8 0.1 broadcast_bitcast_fusion
  12.8 0.9 fusion.10
  13.8 44.2 %collective-permute-done = bf16[512,1024]{1,0:T(8,128)(2,1)S(1)} collective-permute-done((bf16[512,1024]{1,0:T(8,128)(2,1)}, bf16[512,1024]{1,0:T(8,128)(2,1)S(1)}, u32[]{:S(2)}, u32[]{:S(2)}) %collective-permute-start) | collective-permute-done | bytes 1048608 | tf_op jit(solution)/shard_map/ppermute | solution.py:24
  57.9 2.4 broadcast_select_fusion
  60.4 0.0 all-gather.9.cloned.1.call-start
  60.4 0.0 all-gather.7.cloned.1.call-done
  60.5 2.1 convert_reduce_fusion
  62.6 0.1 copy-done.2
  62.7 0.7 fusion.2
  63.4 8.2 %multiply_convert_fusion.4 = (bf16[512,1536]{1,0:T(8,128)(2,1)}, f32[512,1536]{1,0:T(8,128)}) fusion(bf16[2048,1536]{1,0:T(8,128)(2,1)} %param.12, f32[2048]{0:T(1024)S(1)} %copy-done.13, f32[512]{0:T(512)S(1)} %add_rsqrt_fusion.1, f32[512]{0:T(512)S(1)} %broadcast_multiply_fusion.5, bf16[512,2048]{1,0:T(8,128)(2,1)S(1)} %copy-done.2), kind=kOutput, calls=%fused_computation.13 | convolution fusion | flops 3230400512 | bytes 13119488 | tf_op jit(solution)/shard_map/dot_general | solution.py:93
  71.6 2.6 copy.20
  74.2 4.3 %multiply_convert_fusion.1 = (bf16[4,512,512]{2,1,0:T(8,128)(2,1)S(1)}, f32[4,512,512]{2,1,0:T(8,128)}) fusion(f32[512,512]{1,0:T(8,128)S(1)} %fusion.10, bf16[512,4,384]{0,2,1:T(8,128)(2,1)} %bitcast.36), kind=kOutput, calls=%fused_computation.8 | convolution fusion | flops 140509184 | bytes 7864320 | tf_op jit(solution)/shard_map/qhd,khd->hqk/dot_general | solution.py:35
  78.5 1.4 copy-done.5
  79.8 1.9 fusion.24
  81.7 0.1 multiply_reduce_fusion.2
  81.9 12.9 %all-gather.5.cloned.1.call-done = bf16[512,2048]{1,0:T(8,128)(2,1)} async-done(((bf16[512,1024]{1,0:T(8,128)(2,1)}), bf16[512,2048]{1,0:T(8,128)(2,1)}) %all-gather.5.cloned.1.call-update) | async-done | bytes 2097168 | tf_op jit(solution)/shard_map/all_gather | solution.py:84
  94.8 3.0 fusion.25
  97.8 1.2 fusion.16
  99.0 0.4 multiply_convert_fusion.5
  99.4 1.1 copy-done.14
  100.5 2.1 multiply_convert_fusion
  102.6 0.5 convolution_bitcast_fusion.2
  103.1 0.7 convolution_bitcast_fusion.3
  103.8 0.4 copy-done.6
  104.2 0.4 convolution_bitcast_fusion
  104.6 2.0 pad_maximum_fusion
  106.6 3.5 copy.19
  110.1 3.9 multiply_convert_fusion.3
  114.1 1.2 copy-done.10
  115.3 7.7 %convolution_convert_fusion = bf16[512,2048]{1,0:T(8,128)(2,1)} fusion(bf16[512,1536]{1,0:T(8,128)(2,1)S(1)} %multiply_convert_fusion.3, bf16[2048,1536]{1,0:T(8,128)(2,1)} %param.12), kind=kOutput, calls=%fused_computation.15 | convolution fusion | flops 3222274048 | bytes 9961472 | tf_op jit(solution)/shard_map/dot_general | solution.py:114
  123.0 0.0 all-gather.9.cloned.1.call-update
  123.0 0.2 reduce-scatter.5.cloned.1.call-start
  123.3 3.2 fusion.26
  126.5 0.0 reduce-scatter.5.cloned.1.call-update
  126.5 0.0 reduce-scatter.3.cloned.1.call-start
  126.5 1.5 copy-done.3
  128.0 8.5 %fusion.11 = f32[2048,1536]{1,0:T(8,128)} fusion(bf16[512,1536]{1,0:T(8,128)(2,1)} %copy-done.10, f32[2048]{0:T(1024)S(1)} %copy-done.13, bf16[512,2048]{1,0:T(8,128)(2,1)S(1)} %copy-done.3, f32[512]{0:T(512)S(1)} %add_rsqrt_fusion.1, f32[512]{0:T(512)S(1)} %broadcast_multiply_fusion.5), kind=kOutput, calls=%fused_computation.38 | convolution fusion | flops 3226468352 | bytes 16265216 | tf_op jit(solution)/shard_map/dot_general | solution.py:110
  136.6 43.3 %all-gather.9.cloned.1.call-done = bf16[1024,2048]{1,0:T(8,128)(2,1)} async-done(((bf16[512,2048]{1,0:T(8,128)(2,1)}), bf16[1024,2048]{1,0:T(8,128)(2,1)}) %all-gather.9.cloned.1.call-update) | async-done | bytes 4194320 | tf_op jit(solution)/shard_map/all_gather | solution.py:14
  179.9 5.1 %reduce_sum.90 = bf16[512,2048]{1,0:T(8,128)(2,1)} reduce(bf16[2,512,2048]{2,1,0:T(8,128)(2,1)} %bitcast.43, bf16[]{:T(256)} %constant.29.clone.1), dimensions={0}, to_apply=%region_6.7 | reduce | flops 1048576 | bytes 6291458 | tf_op jit(solution)/shard_map/reduce_sum | solution.py:14
  185.0 3.0 fusion.7
  188.1 1.5 fusion.6
  189.6 67.5 %reduce-scatter.5.cloned.1.call-done = f32[512,128]{1,0:T(8,128)} async-done(((f32[512,2048]{1,0:T(8,128)}), f32[512,128]{1,0:T(8,128)}) %reduce-scatter.5.cloned.1.call-update) | async-done | bytes 262160 | tf_op jit(solution)/shard_map/reduce_scatter | solution.py:108
  257.0 138.4 %reduce-scatter.3.cloned.1.call-done = f32[128,1536]{1,0:T(8,128)} async-done(((f32[2048,1536]{1,0:T(8,128)}), f32[128,1536]{1,0:T(8,128)}) %reduce-scatter.3.cloned.1.call-update) | async-done | bytes 786448 | tf_op jit(solution)/shard_map/reduce_scatter | solution.py:113
  (33 shorter events, 0.1 us)
Async XLA Ops:
  7.2 87.6 %copy-start = (bf16[512,2048]{1,0:T(8,128)(2,1)S(1)}, bf16[512,2048]{1,0:T(8,128)(2,1)}, u32[]{:S(2)}) copy-start(bf16[512,2048]{1,0:T(8,128)(2,1)} %param.13) | copy-start | bytes 6291460
  7.2 53.3 %all-gather.7.cloned.1.call-start = ((), (), s32[]{:S(2)}) async-start(), calls=%async_computation.3 | async-start | bytes 3145728 | tf_op jit(solution)/shard_map/all_gather | solution.py:83
  7.9 86.9 %all-gather.5.cloned.1.call-start = ((), (), s32[]{:S(2)}) async-start(), calls=%async_computation.2 | async-start | bytes 3145728 | tf_op jit(solution)/shard_map/all_gather | solution.py:84
  8.0 50.0 %collective-permute-start = (bf16[512,1024]{1,0:T(8,128)(2,1)}, bf16[512,1024]{1,0:T(8,128)(2,1)S(1)}, u32[]{:S(2)}, u32[]{:S(2)}) collective-permute-start(bf16[512,1024]{1,0:T(8,128)(2,1)} %param.8), channel_id=1, source_target_pairs={{0,16},{16,0},{2,18},{18,2},{4,20},{20,4},{6,22},{22,6},{8,24},{24... | collective-permute-start | bytes 3145736 | tf_op jit(solution)/shard_map/ppermute | solution.py:24
  13.8 60.4 %copy-start.11 = (f32[512,512]{1,0:T(8,128)}, f32[512,512]{1,0:T(8,128)S(1)}, u32[]{:S(2)}) copy-start(f32[512,512]{1,0:T(8,128)S(1)} %fusion.10) | copy-start | bytes 3145732
  60.3 3.0 copy-start.13
  60.4 119.5 %all-gather.9.cloned.1.call-start = ((), (), s32[]{:S(2)}) async-start(), calls=%async_computation.6 | async-start | bytes 6291456 | tf_op jit(solution)/shard_map/all_gather | solution.py:14
  60.4 2.2 copy-start.2
  78.5 1.4 copy-start.5
  94.8 3.0 copy-start.4
  97.8 1.6 copy-start.12
  97.8 2.7 copy-start.14
  102.6 1.6 copy-start.6
  114.1 1.2 copy-start.10
  115.3 7.9 %copy-start.7 = (bf16[512,2048]{1,0:T(8,128)(2,1)S(1)}, bf16[512,2048]{1,0:T(8,128)(2,1)}, u32[]{:S(2)}) copy-start(bf16[512,2048]{1,0:T(8,128)(2,1)} %all-gather.5.cloned.1.call-done) | copy-start | bytes 6291460
  115.3 8.0 %copy-start.9 = (bf16[512,4,128]{0,2,1:T(8,128)(2,1)S(1)}, bf16[512,4,128]{0,2,1:T(8,128)(2,1)}, u32[]{:S(2)}) copy-start(bf16[512,4,128]{0,2,1:T(8,128)(2,1)} %get-tuple-element.7) | copy-start | bytes 1572868
  123.0 134.0 %reduce-scatter.5.cloned.1.call-start = ((), (), s32[]{:S(2)}) async-start(), calls=%async_computation.5 | async-start | bytes 4456448 | tf_op jit(solution)/shard_map/reduce_scatter | solution.py:108
  126.5 1.6 copy-start.3
  126.5 269.0 %reduce-scatter.3.cloned.1.call-start = ((), (), s32[]{:S(2)}) async-start(), calls=%async_computation.4 | async-start | bytes 13369344 | tf_op jit(solution)/shard_map/reduce_scatter | solution.py:113
  185.0 3.1 copy-start.8
  188.0 207.4 %copy-start.1 = (bf16[512,2048]{1,0:T(8,128)(2,1)S(1)}, bf16[512,2048]{1,0:T(8,128)(2,1)}, u32[]{:S(2)}) copy-start(bf16[512,2048]{1,0:T(8,128)(2,1)} %param.13) | copy-start | bytes 6291460
Sparse Core Ops, SparseCore 0:
  9.5 35.8 all-gather.6
  60.5 34.2 all-gather.4
  123.1 56.7 all-gather.8
  184.2 72.8 reduce-scatter.4
  261.5 133.9 reduce-scatter.2
